TPU v7x, 256 devices: a whole 4x4x8 slice. The times are simulated.
256 devices in a mesh: samples: 256 (over y, z, x, core).
Axes of the slice: x: 4, y: 4, z: 8, core: 2. Of those that a mesh axis runs over, the one named last changes fastest.
Arguments:
- spin_configs: int32 [256, 256], P('samples'), may hold values from -1 to 1, as said below
- energy: float32 [256], P('samples'), may hold values from -6 to 6
- embedding: float32 [9, 64], replicated, may hold values from -2 to 2
- kernels: float32 [24, 9, 64, 64], replicated, may hold values from -0.25 to 0.25
- readout: float32 [64], replicated, may hold values from -0.75 to 0.75
Outputs:
- update_step: float32 [884736], P('samples')
Inputs may be any that keep to these rules, and one draw needn't show every extreme that they name: `spin_configs`: every entry is +1 or -1, and each sample has as many +1 as -1 entries.
All inputs are finite; a program needn't handle non-finite values.
Results may differ from a plain program's by a relative error of at most 0.004.
The roundings to bfloat16 on the way count: a program that leaves them out, or rounds other values in their place, can miss the bound.
Values may be sent and summed in bfloat16 or wider, within the bound.
No kernel may reach another device: no remote copies, remote signals or barrier semaphores. Data moves between devices by JAX's collectives and lax.ppermute only.
A program may use at most 128 MiB of HBM per device.

v0:
```python
import math
import jax
import jax.numpy as jnp
from jax import lax
from jax.sharding import PartitionSpec as P

SIDE = 16
shift_ratio = 0.05


def shifted_copies(values, lattice_side):
    channels = values.shape[0]
    lattice = values.reshape(channels, lattice_side, lattice_side)
    copies = [
        jnp.roll(lattice, (row_step, col_step), axis=(1, 2))
        for row_step in (1, 0, -1)
        for col_step in (1, 0, -1)
    ]
    return jnp.stack(copies, 0).reshape(9, channels, lattice_side * lattice_side)


def layer_norm(values):
    deviation = values - jnp.mean(values, axis=0, keepdims=True)
    return deviation * lax.rsqrt(jnp.mean(deviation * deviation, axis=0, keepdims=True) + 1e-05)


def block_step(hidden, kernel, lattice_side):
    active = jax.nn.gelu(layer_norm(hidden))
    return hidden + jnp.einsum(
        "kis,kio->os", shifted_copies(active, lattice_side), kernel, precision=lax.Precision.HIGHEST
    )


def log_amplitude(all_kernels, spin_row, embedding, readout, lattice_side):
    spin_field = spin_row.astype(jnp.float32)[None, :]
    hidden = jnp.einsum(
        "kcs,kcd->ds",
        shifted_copies(spin_field, lattice_side),
        embedding[:, None, :],
        precision=lax.Precision.HIGHEST,
    )
    hidden, unused = lax.scan(
        lambda carry, kernel: (block_step(carry, kernel, lattice_side), None), hidden, all_kernels
    )
    return jnp.sum(readout[:, None] * jax.nn.gelu(layer_norm(hidden))) / lattice_side


def solve_coeffs(gram_matrix, energy_all):
    sample_count = gram_matrix.shape[0]
    spread = (energy_all - jnp.mean(energy_all)) / math.sqrt(sample_count)
    diag_term = shift_ratio * jnp.mean(jnp.diagonal(gram_matrix)) + 1e-06
    system = gram_matrix + diag_term * jnp.eye(sample_count, dtype=jnp.float32)
    factor = jnp.linalg.cholesky(system)
    return jax.scipy.linalg.cho_solve((factor, True), spread)


def per_device(spin_configs, energy, embedding, kernels, readout):
    samples_here = spin_configs.shape[0]
    gradient = jax.grad(
        lambda all_kernels, spin_row: log_amplitude(all_kernels, spin_row, embedding, readout, SIDE)
    )
    logderiv = jax.vmap(gradient, in_axes=(None, 0))(kernels, spin_configs).reshape(
        samples_here, -1
    )
    full_len = logderiv.shape[1]
    sample_count = samples_here * lax.axis_size("samples")
    grad_total = lax.psum(jnp.sum(logderiv, axis=0), "samples")
    mean_row = grad_total / sample_count
    centered = ((logderiv - mean_row) / math.sqrt(sample_count)).astype(jnp.bfloat16)
    columns = lax.all_to_all(centered, "samples", split_axis=1, concat_axis=0, tiled=True)
    partial_gram = lax.dot_general(
        columns, columns, (((1,), (1,)), ((), ())), preferred_element_type=jnp.float32
    )
    gram_matrix = lax.psum(partial_gram, "samples")
    energy_all = lax.all_gather(energy, "samples", axis=0, tiled=True)
    coeffs = solve_coeffs(gram_matrix, energy_all)
    own_part = jnp.dot(coeffs, columns.astype(jnp.float32), precision=lax.Precision.HIGHEST)
    square_total = lax.psum(jnp.sum(own_part * own_part), "samples")
    return own_part * lax.rsqrt(square_total / full_len + 1e-06)


def solution(mesh):
    return jax.shard_map(
        per_device,
        mesh=mesh,
        in_specs=(P("samples", None), P("samples"), P(), P(), P()),
        out_specs=P("samples"),
        check_vma=False,
    )
```

profile of v0, /device:TPU:1, one launch (start us, length us, event | category | flops | bytes accessed | tf_op | source)
XLA Modules:
  0.0 1202.7 jit_solution(16037261148835651161)
XLA Ops:
  9.8 134.3 %while.43 = (s32[]{:T(128)}, f32[1,64,256]{2,1,0:T(8,128)S(1)}, f32[24,1,64,256]{3,2,1,0:T(8,128)}, f32[24,1,1,256]{3,2,1,0:T(1,128)S(1)}, f32[24,1,1,256]{3,2,1...) while((s32[]{:T(128)}, f32[1,64,256]{2,1,0:T(8,128)S(1)}, ...), condition=%wide.region_3.4_spmd, body=%wide.region_0.3_spmd.sunk | while | flops 114213632 | bytes 9556613 | solution.py:42
  144.6 3.7 broadcast_in_dim.88
  148.3 228.3 %while.44 = (s32[]{:T(128)}, f32[1,64,256]{1,2,0:T(8,128)S(1)}, f32[24,1,9,64,64]{4,3,2,1,0:T(8,128)}, f32[24,9,64,64]{3,2,1,0:T(8,128)}, f32[24,1,64,256]{3,2,1...) while((s32[]{:T(128)}, f32[1,64,256]{1,2,0:T(8,128)S(1)}, ...), condition=%wide.region_11.12_spmd, body=%wide.region_8.11_spmd.sunk | while | flops 227329024 | bytes 7526585 | solution.py:42
  164.7 2.4 fusion.151
  174.2 2.4 fusion.151
  193.3 2.4 fusion.151
  202.8 2.4 fusion.151
  221.8 2.4 fusion.151
  231.4 2.4 fusion.151
  250.4 2.4 fusion.151
  297.9 2.4 fusion.151
  326.5 2.4 fusion.151
  336.0 2.4 fusion.151
  355.0 2.4 fusion.151
  376.6 6.8 transpose.94
  383.5 270.7 %all-reduce.29.cloned.1.call-done = f32[884736]{0:T(1024)} async-done(((f32[884736]{0:T(1024)}), f32[884736]{0:T(1024)}) %all-reduce.29.cloned.1.call-update) | async-done | bytes 3538960 | tf_op jit(solution)/shard_map/psum | solution.py:67
  654.2 3.7 multiply_convert_fusion
  657.9 7.5 all_to_all.15
  666.1 12.0 reduce.50
  678.0 5.5 reshape.752
  683.5 13.2 %all-to-all-start = ((bf16[256,2,1728]{2,1,0:T(2,128)(2,1)}), bf16[256,2,1728]{2,1,0:T(2,128)(2,1)}, u32[]{:S(2)}, u32[]{:S(2)}) async-start(bf16[256,2,1728]{2,1,0:T(2,128)(2,1)} %reshape.752), calls=%async_computation | async-start | bytes 3670016 | tf_op jit(solution)/shard_map/all_to_all | solution.py:70
  697.5 85.0 %all-reduce.25 = f32[256]{0:T(256)S(1)} all-reduce(f32[256]{0:T(256)S(1)} %dynamic-update-slice.11), channel_id=1, replica_groups=mesh['samples'=256] {'samples'}, use_global_device_ids=true, to_apply=%add.25 | all-reduce | flops 256 | bytes 2048
  783.7 11.1 reshape.753
  796.7 250.1 %all-reduce.31.cloned.1.call-done = f32[256,256]{0,1:T(8,128)} async-done(((f32[256,256]{0,1:T(8,128)}), f32[256,256]{0,1:T(8,128)}) %all-reduce.31.cloned.1.call-update) | async-done | bytes 262160 | tf_op jit(solution)/shard_map/psum | solution.py:74
  1046.8 2.7 gather_fusion
  1051.9 11.7 cholesky.49
  1063.7 9.8 custom-call.18
  1074.0 11.7 cholesky.103
  1088.6 4.1 while.45
  1092.7 19.7 %custom-call.19 = f32[2,128,128]{1,2,0:T(8,128)S(1)} custom-call(f32[2,128,128]{2,1,0:T(8,128)S(1)} %get-tuple-element.324), custom_call_target="InvertDiagBlocksLowerTriangular" | custom-call | tf_op jit(solution)/shard_map/jit(_cho_solve)/triangular_solve | solution.py:54
  1113.5 2.9 fusion.49
  1117.0 77.6 %psum.23 = f32[]{:T(128)} all-reduce(f32[]{:T(128)} %multiply_reduce_fusion.3), channel_id=1, replica_groups=mesh['samples'=256] {'samples'}, use_global_device_ids=true, to_apply=%region_21.22 | all-reduce | flops 1 | bytes 8 | tf_op jit(solution)/shard_map/psum | solution.py:78
  (2431 shorter events, 337.9 us)
Async XLA Ops:
  6.5 3.0 copy-start
  6.5 647.6 %all-reduce.29.cloned.1.call-start = ((), (), s32[]{:S(2)}) async-start(), calls=%async_computation.1 | async-start | bytes 7077888 | tf_op jit(solution)/shard_map/psum | solution.py:67
  9.8 134.5 %copy-start.5 = (f32[64]{0:T(128)S(1)}, f32[64]{0:T(128)}, u32[]{:S(2)}) copy-start(f32[64]{0:T(128)} %param.13) | copy-start | bytes 772
  383.5 270.7 %copy-start.2 = (f32[884736]{0:T(1024)S(1)}, f32[884736]{0:T(1024)}, u32[]{:S(2)}) copy-start(f32[884736]{0:T(1024)} %transpose.94) | copy-start | bytes 10616836
  683.5 100.2 %all-to-all-start = ((bf16[256,2,1728]{2,1,0:T(2,128)(2,1)}), bf16[256,2,1728]{2,1,0:T(2,128)(2,1)}, u32[]{:S(2)}, u32[]{:S(2)}) async-start(bf16[256,2,1728]{2,1,0:T(2,128)(2,1)} %reshape.752), calls=%async_computation | async-start | bytes 3670016 | tf_op jit(solution)/shard_map/all_to_all | solution.py:70
  696.7 350.1 %all-reduce.31.cloned.1.call-start = ((), (), s32[]{:S(2)}) async-start(), calls=%async_computation.2 | async-start | bytes 524288 | tf_op jit(solution)/shard_map/psum | solution.py:74
  794.9 1.8 copy-start.4
  1046.8 5.1 copy-start.3
  1088.6 107.3 %copy-start.1 = (f32[9,64]{1,0:T(8,128)S(1)}, f32[9,64]{1,0:T(8,128)}, u32[]{:S(2)}) copy-start(f32[9,64]{1,0:T(8,128)} %param.11) | copy-start | bytes 6916
Sparse Core Ops, SparseCore 0:
  383.6 270.5 all-reduce.28
  796.8 249.9 all-reduce.30
where the time goes:
time: 1210 us; the launch traced here: 1200 us
  waiting for transfers between devices  521 us (43%)
  local copies, waits for them, and re-layouts  196 us (16%)
  blocking collectives  163 us (13%)
  matrix products  154 us (13%)
  other arithmetic  123 us (10%)
  between operations  17.4 us (1%)
  loops' own time  15.4 us (1%)
  starting transfers between devices  13.2 us (1%)
    psum x1, waiting for transfers between devices, per_device(): grad_total = lax.psum(jnp.sum(logderiv, axis=0), 'samples')  271 us
    psum x1, waiting for transfers between devices, per_device(): gram_matrix = lax.psum(partial_gram, 'samples')  250 us
    dot_general x72, matrix products, block_step(): jnp.einsum('kis,kio->os', shifted_copies(active, lattice_side), kernel, p...  148 us
    unnamed x1, blocking collectives  85 us
    dynamic_slice x240, local copies, waits for them, and re-layouts, log_amplitude(): lax.scan(lambda carry, kernel: (block_step(carry, kernel, lattice_side),...  83.2 us
    psum x1, blocking collectives, per_device(): square_total = lax.psum(jnp.sum(own_part * own_part), 'samples')  77.6 us
    another operation x7, other arithmetic, solve_coeffs(): factor = jnp.linalg.cholesky(system)  34.5 us
    another operation x465, local copies, waits for them, and re-layouts, shifted_copies(): jnp.stack(copies, 0).reshape(9, channels, lattice_side * lattice_side)  32.6 us
  transfers between devices with their start and end apart: 3, of which 2 were waited for; matrix products, arithmetic and copies ran while one was open for 0% of the time, Pallas kernels for 0%

commit v1 on v0

--- a/solution.py
+++ b/solution.py
@@ -71,7 +71,7 @@
     partial_gram = lax.dot_general(
         columns, columns, (((1,), (1,)), ((), ())), preferred_element_type=jnp.float32
     )
-    gram_matrix = lax.psum(partial_gram, "samples")
+    gram_matrix = jnp.sum(lax.all_gather(partial_gram, "samples"), axis=0)
     energy_all = lax.all_gather(energy, "samples", axis=0, tiled=True)
     coeffs = solve_coeffs(gram_matrix, energy_all)
     own_part = jnp.dot(coeffs, columns.astype(jnp.float32), precision=lax.Precision.HIGHEST)

time: 1210 us -> 1170 us (0.967)
  waiting for transfers between devices: 521 us -> 400 us
  blocking collectives: 163 us -> 209 us
  other arithmetic: 123 us -> 145 us
  local copies, waits for them, and re-layouts: 196 us -> 217 us
  starting transfers between devices: 13.2 us -> 0.04 us
    psum x1 -> x0, waiting for transfers between devices: 250 us -> none  [per_device(): gram_matrix = lax.psum(partial_gram, 'samples')]
    all_gather x0 -> x1, waiting for transfers between devices: none -> 130 us  [per_device(): gram_matrix = jnp.sum(lax.all_gather(partial_gram, 'samples'), axis=0)]
    all_to_all x0 -> x1, blocking collectives: none -> 60.1 us  [per_device(): lax.all_to_all(centered, 'samples', split_axis=1, concat_axis=0, tiled=True)]
    reduce_sum x0 -> x1, other arithmetic: none -> 21 us  [per_device(): gram_matrix = jnp.sum(lax.all_gather(partial_gram, 'samples'), axis=0)]
    dynamic_slice x240, local copies, waits for them, and re-layouts: 83.2 us -> 104 us  [log_amplitude(): lax.scan(lambda carry, kernel: (block_step(carry, kernel, lattice_side),...]
    all_to_all x1 -> x0, starting transfers between devices: 13.2 us -> none  [per_device(): lax.all_to_all(centered, 'samples', split_axis=1, concat_axis=0, tiled=True)]
  transfers between devices with their start and end apart: 3 -> 2, of which waited for: 2 -> 2; matrix products, arithmetic and copies ran while one was open for 0% -> 0% of each run, Pallas kernels for 0% -> 0%
where the time goes in v1:
time: 1170 us; the launch traced here: 1160 us
  waiting for transfers between devices  400 us (34%)
  local copies, waits for them, and re-layouts  217 us (19%)
  blocking collectives  209 us (18%)
  matrix products  154 us (13%)
  other arithmetic  145 us (12%)
  between operations  17.6 us (2%)
  loops' own time  14.8 us (1%)
    psum x1, waiting for transfers between devices, per_device(): grad_total = lax.psum(jnp.sum(logderiv, axis=0), 'samples')  271 us
    dot_general x72, matrix products, block_step(): jnp.einsum('kis,kio->os', shifted_copies(active, lattice_side), kernel, p...  147 us
    all_gather x1, waiting for transfers between devices, per_device(): gram_matrix = jnp.sum(lax.all_gather(partial_gram, 'samples'), axis=0)  130 us
    dynamic_slice x240, local copies, waits for them, and re-layouts, log_amplitude(): lax.scan(lambda carry, kernel: (block_step(carry, kernel, lattice_side),...  104 us
    unnamed x1, blocking collectives  75.1 us
    psum x1, blocking collectives, per_device(): square_total = lax.psum(jnp.sum(own_part * own_part), 'samples')  74.3 us
    all_to_all x1, blocking collectives, per_device(): lax.all_to_all(centered, 'samples', split_axis=1, concat_axis=0, tiled=True)  60.1 us
    another operation x7, other arithmetic, solve_coeffs(): factor = jnp.linalg.cholesky(system)  34.6 us
  transfers between devices with their start and end apart: 2, of which 2 were waited for; matrix products, arithmetic and copies ran while one was open for 0% of the time, Pallas kernels for 0%

profile of v1, /device:TPU:1, one launch (start us, length us, event | category | flops | bytes accessed | tf_op | source)
XLA Modules:
  0.0 1158.0 jit_solution(5085949024064794166)
XLA Ops:
  9.8 135.1 %while.43 = (s32[]{:T(128)}, f32[1,64,256]{2,1,0:T(8,128)S(1)}, f32[24,1,64,256]{3,2,1,0:T(8,128)}, f32[24,1,1,256]{3,2,1,0:T(1,128)S(1)}, f32[24,1,1,256]{3,2,1...) while((s32[]{:T(128)}, f32[1,64,256]{2,1,0:T(8,128)S(1)}, ...), condition=%wide.region_3.4_spmd, body=%wide.region_0.3_spmd.sunk | while | flops 114213632 | bytes 9556613 | solution.py:42
  145.3 3.7 broadcast_in_dim.88
  149.1 248.8 %while.44 = (s32[]{:T(128)}, f32[1,64,256]{1,2,0:T(8,128)S(1)}, f32[24,1,9,64,64]{4,3,2,1,0:T(8,128)}, f32[24,9,64,64]{3,2,1,0:T(8,128)}, f32[24,1,64,256]{3,2,1...) while((s32[]{:T(128)}, f32[1,64,256]{1,2,0:T(8,128)S(1)}, ...), condition=%wide.region_11.12_spmd, body=%wide.region_8.11_spmd.sunk | while | flops 227329024 | bytes 7526585 | solution.py:42
  167.2 2.4 fusion.150
  177.5 2.4 fusion.150
  198.3 2.4 fusion.150
  208.7 2.4 fusion.150
  229.4 2.4 fusion.150
  239.8 2.4 fusion.150
  260.5 2.4 fusion.150
  312.3 2.4 fusion.150
  343.4 2.4 fusion.150
  353.8 2.4 fusion.150
  374.6 2.4 fusion.150
  397.9 6.8 transpose.93
  404.8 270.6 %all-reduce.28.cloned.1.call-done = f32[884736]{0:T(1024)} async-done(((f32[884736]{0:T(1024)}), f32[884736]{0:T(1024)}) %all-reduce.28.cloned.1.call-update) | async-done | bytes 3538960 | tf_op jit(solution)/shard_map/psum | solution.py:67
  675.4 3.6 multiply_convert_fusion
  679.0 7.5 all_to_all.15
  687.1 11.9 %reduce.50 = bf16[256,3456]{1,0:T(8,128)(2,1)} reduce(bf16[256,1,3456]{2,1,0:T(2,128)(2,1)S(1)} %bitcast.381, bf16[]{:T(256)} %broadcast.690), dimensions={1}, to_apply=%bitcast.236.reduce_sub_computation | reduce | bytes 3538946
  699.0 4.7 reshape.753
  703.8 60.1 %all_to_all.17 = bf16[256,2,1728]{2,1,0:T(2,128)(2,1)} all-to-all(bf16[256,2,1728]{2,1,0:T(2,128)(2,1)S(1)} %reshape.753), channel_id=1, replica_groups=mesh['samples'=256] {'samples'}, dimensions={0} | all-to-all | bytes 3538944 | tf_op jit(solution)/shard_map/all_to_all | solution.py:70
  763.8 11.1 reshape.754
  777.6 75.1 %all-reduce.25 = f32[256]{0:T(256)S(1)} all-reduce(f32[256]{0:T(256)S(1)} %dynamic-update-slice.11), channel_id=1, replica_groups=mesh['samples'=256] {'samples'}, use_global_device_ids=true, to_apply=%add.25 | all-reduce | flops 256 | bytes 2048
  854.0 129.6 %all-gather.3.cloned.1.call-done = f32[65536,256]{1,0:T(8,128)} async-done(((f32[256,256]{1,0:T(8,128)}), f32[65536,256]{1,0:T(8,128)}) %all-gather.3.cloned.1.call-update) | async-done | bytes 67108880 | tf_op jit(solution)/shard_map/all_gather | solution.py:74
  983.6 21.0 %reduce_sum.136 = f32[256,256]{1,0:T(8,128)S(1)} reduce(f32[256,256,256]{2,1,0:T(8,128)} %bitcast.67, f32[]{:T(128)} %constant.267.clone.1), dimensions={0}, to_apply=%region_13.14 | reduce | flops 16711680 | bytes 67371008 | tf_op jit(solution)/shard_map/reduce_sum | solution.py:74
  1008.6 11.7 %cholesky.49 = f32[128,128]{1,0:T(8,128)S(1)} custom-call(f32[128,128]{1,0:T(8,128)S(1)} %cholesky.115), custom_call_target="Cholesky" | custom-call | tf_op jit(solution)/shard_map/jit(cholesky)/cholesky | solution.py:53
  1020.3 9.8 custom-call.18
  1030.6 11.7 %cholesky.103 = f32[128,128]{1,0:T(8,128)S(1)} custom-call(f32[128,128]{1,0:T(8,128)S(1)} %convolution_subtract_fusion), custom_call_target="Cholesky" | custom-call | tf_op jit(solution)/shard_map/jit(cholesky)/cholesky | solution.py:53
  1045.1 5.3 while.45
  1050.4 20.5 %custom-call.19 = f32[2,128,128]{1,2,0:T(8,128)S(1)} custom-call(f32[2,128,128]{2,1,0:T(8,128)} %get-tuple-element.324), custom_call_target="InvertDiagBlocksLowerTriangular" | custom-call | tf_op jit(solution)/shard_map/jit(_cho_solve)/triangular_solve | solution.py:54
  1072.0 2.9 fusion.49
  1075.5 74.3 %psum.15 = f32[]{:T(128)} all-reduce(f32[]{:T(128)} %multiply_reduce_fusion.3), channel_id=1, replica_groups=mesh['samples'=256] {'samples'}, use_global_device_ids=true, to_apply=%region_21.22 | all-reduce | flops 1 | bytes 8 | tf_op jit(solution)/shard_map/psum | solution.py:78
  (2419 shorter events, 362.1 us)
Async XLA Ops:
  6.5 3.0 copy-start
  6.5 668.9 %all-reduce.28.cloned.1.call-start = ((), (), s32[]{:S(2)}) async-start(), calls=%async_computation.1 | async-start | bytes 7077888 | tf_op jit(solution)/shard_map/psum | solution.py:67
  9.8 135.2 %copy-start.4 = (f32[64]{0:T(128)S(1)}, f32[64]{0:T(128)}, u32[]{:S(2)}) copy-start(f32[64]{0:T(128)} %param.13) | copy-start | bytes 772
  404.7 270.7 %copy-start.2 = (f32[884736]{0:T(1024)S(1)}, f32[884736]{0:T(1024)}, u32[]{:S(2)}) copy-start(f32[884736]{0:T(1024)} %transpose.93) | copy-start | bytes 10616836
  404.8 578.8 %all-gather.3.cloned.1.call-start = ((), (), s32[]{:S(2)}) async-start(), calls=%async_computation.2 | async-start | bytes 67371008 | tf_op jit(solution)/shard_map/all_gather | solution.py:74
  775.0 79.0 %copy-start.3 = (bf16[256,1,3456]{2,1,0:T(2,128)(2,1)}, bf16[256,1,3456]{2,1,0:T(2,128)(2,1)S(1)}, u32[]{:S(2)}) copy-start(bf16[256,1,3456]{2,1,0:T(2,128)(2,1)S(1)} %reshape.754) | copy-start | bytes 5308420
  1045.0 106.2 %copy-start.1 = (f32[9,64]{1,0:T(8,128)S(1)}, f32[9,64]{1,0:T(8,128)}, u32[]{:S(2)}) copy-start(f32[9,64]{1,0:T(8,128)} %param.11) | copy-start | bytes 6916
Sparse Core Ops, SparseCore 0:
  404.9 270.4 all-reduce.27
  777.0 206.5 all-gather.2
